TPU v7x, 32 devices: a whole 2x2x4 slice. The times are simulated.
32 devices in a mesh: rows: 8 (over z, y), cols: 4 (over x, core).
Axes of the slice: x: 2, y: 2, z: 4, core: 2. Of those that a mesh axis runs over, the one named last changes fastest.
Arguments:
- sketch: float32 [32768, 256], P(('rows', 'cols'))
- tiles: bfloat16 [1280, 512, 512], P(('rows', 'cols')), may hold values from -48 to 48
- tile_user: int32 [1280], P(('rows', 'cols')), may hold values from 0 to 7
- tile_item: int32 [1280], P(('rows', 'cols')), may hold values from 0 to 7
- tile_count: int32 [32], P(('rows', 'cols')), may hold values from 5 to 40, as said below
- item_owner: int32 [4, 8], P('cols'), may hold values from 0 to 7, each once within a row
Outputs:
- projected: float32 [8, 4, 256, 512], P('rows', 'cols')
Inputs may be any that keep to these rules, and one draw needn't show every extreme that they name: `tile_count`: live slots of a device are its first slots; some device has all 40 live in every draw.
All inputs are finite; a program needn't handle non-finite values.
Results may differ from a plain program's by a relative error of at most 0.0029.
Values may be sent and summed in bfloat16 or wider, within the bound.
No kernel may reach another device: no remote copies, remote signals or barrier semaphores. Data moves between devices by JAX's collectives and lax.ppermute only.
A program may use at most 192 MiB of HBM per device.

v0:
```python
import functools

import jax
import jax.numpy as jnp
from jax import lax
from jax.experimental import pallas as pl
from jax.experimental.pallas import tpu as pltpu
from jax.sharding import PartitionSpec as P

F32 = jnp.float32
BF16 = jnp.bfloat16
HIGH = lax.Precision.HIGHEST
SLOTS = 12
SPARE = 4 * 2**20
GROUP = 4
NEAR_COST = 200 * 2**20
EARLY_COST = 1024
LATE_COST = 1024
FACTOR_COST = 200 * 2**20
CHUNKS = (160, 96)
NEWTON = 2


def bits_of(count):
    return [1 << b for b in reversed(range(count.bit_length() - 1))]


def swap(x, axis, count, bit):
    return lax.ppermute(x, axis, [(i, i ^ bit) for i in range(count)])


def places(order, parity):
    found = [parity << order[0]]
    for bit in reversed(order[1:]):
        found = found + [p | (1 << bit) for p in found]
    return found


def run_tiles(base, span, per_piece, users, items, owner, meta, tiles, slab, add, buf, sems, order):
    count, row, col = meta[0], meta[1], meta[2]

    def relative(t):
        user = users[t]
        return lax.bitwise_xor(user // per_piece, col) - base, lax.rem(user, per_piece)

    def choose(t, n):
        piece, _ = relative(t)
        order[n] = t
        return n + jnp.where((piece >= 0) & (piece < span), 1, 0)

    live = lax.fori_loop(0, count, choose, 0)

    def fetch(i):
        slot = lax.rem(i, SLOTS)
        return pltpu.make_async_copy(tiles.at[order[i]], buf.at[slot], sems.at[slot])

    for i in range(SLOTS):
        @pl.when(i < live)
        def _():
            fetch(i).start()

    def group(first, size):
        for q in range(size):
            fetch(first + q).wait()
        found = []
        for q in range(size):
            piece, part = relative(order[first + q])
            both = jnp.dot(
                slab[piece * per_piece + part],
                buf[lax.rem(first + q, SLOTS)],
                preferred_element_type=F32,
            )
            found.append(both)
        for q in range(size):
            add(lax.bitwise_xor(owner[items[order[first + q]]], row), found[q])
        for q in range(size):
            @pl.when(first + q + SLOTS < live)
            def _():
                fetch(first + q + SLOTS).start()

    def finish():
        groups = live // GROUP

        def many(g, _):
            group(g * GROUP, GROUP)
            return 0

        def one(i, _):
            group(i, 1)
            return 0

        lax.fori_loop(0, groups, many, 0)
        lax.fori_loop(groups * GROUP, live, one, 0)

    return finish


def split_kernel(sketch, flat, *chunks):
    flat[...] = sketch[...].T
    first = 0
    for chunk in chunks:
        kc = chunk.shape[0] // 2
        rows = flat[first : first + kc, :]
        high = rows.astype(BF16)
        chunk[:kc, :] = high
        chunk[kc:, :] = (rows - high.astype(F32)).astype(BF16)
        first += kc


def split_sketch(sketch):
    users, width = sketch.shape
    vmem = pl.BlockSpec(memory_space=pltpu.VMEM)
    return pl.pallas_call(
        split_kernel,
        out_shape=[jax.ShapeDtypeStruct((width, users), F32)]
        + [jax.ShapeDtypeStruct((2 * k, users), BF16) for k in CHUNKS],
        in_specs=[vmem],
        out_specs=[vmem] * (1 + len(CHUNKS)),
        compiler_params=pltpu.CompilerParams(vmem_limit_bytes=16 * 2**20),
    )(sketch)


def gram_kernel(flat, packed):
    n = packed.shape[1]
    top, low = flat[:n, :], flat[n:, :]
    second = mmt(low, low)
    r = lax.broadcasted_iota(jnp.int32, (n, n), 0)
    c = lax.broadcasted_iota(jnp.int32, (n, n), 1)
    packed[:n] = jnp.where(r >= c, mmt(top, top), second)
    packed[n : 2 * n] = mmt(low, top)
    tail = jnp.sum(jnp.where(r == c, second, 0.0), axis=0, keepdims=True)
    packed[2 * n :] = jnp.broadcast_to(tail, (8, n))


def packed_gram(flat):
    n = flat.shape[0] // 2
    vmem = pl.BlockSpec(memory_space=pltpu.VMEM)
    return pl.pallas_call(
        gram_kernel,
        out_shape=jax.ShapeDtypeStruct((2 * n + 8, n), F32),
        in_specs=[vmem],
        out_specs=vmem,
        compiler_params=pltpu.CompilerParams(vmem_limit_bytes=16 * 2**20),
    )(flat)


def fill(slab, pieces, per_piece):
    tile_size = slab.shape[2]
    for c, blocks in enumerate(pieces):
        first = 0
        for block in blocks:
            stop = first + block.shape[0]
            for h in range(per_piece):
                slab[c * per_piece + h, first:stop, :] = block[:, h * tile_size : (h + 1) * tile_size]
            first = stop


def near_kernel(span, blocks, users, items, owner, meta, *refs):
    pieces = [refs[i * blocks : (i + 1) * blocks] for i in range(span)]
    tiles = refs[span * blocks]
    sums = refs[span * blocks + 1 : -4]
    slab, buf, sems, order = refs[-4:]
    per_piece = refs[0].shape[1] // tiles.shape[1]

    def add(place, both):
        first = 0
        for part in sums:
            kc = part.shape[1]
            part[place] += both[first : first + kc] + both[first + kc : first + 2 * kc]
            first += 2 * kc

    finish = run_tiles(
        0, span, per_piece, users, items, owner, meta, tiles, slab, add, buf, sems, order
    )
    for part in sums:
        part[...] = jnp.zeros_like(part)
    fill(slab, pieces, per_piece)
    finish()


def far_kernel(span, blocks, orders, users, items, owner, meta, *refs):
    pieces = [refs[i * blocks : (i + 1) * blocks] for i in range(span)]
    start, tiles = refs[span * blocks], refs[span * blocks + 1]
    outs = refs[span * blocks + 2 : -5]
    slab, buf, sems, order, acc = refs[-5:]
    tile_size = tiles.shape[1]
    per_piece = refs[0].shape[1] // tile_size
    kc = start.shape[1]

    def add(place, both):
        acc[place] += both[:kc] + both[kc:]

    finish = run_tiles(
        span, span, per_piece, users, items, owner, meta, tiles, slab, add, buf, sems, order
    )
    acc[...] = start[...]
    fill(slab, pieces, per_piece)
    finish()
    width = tile_size // len(orders)
    for o, bits in enumerate(orders):
        cut = slice(o * width, (o + 1) * width)
        for k, place in enumerate(places(bits, 0)):
            outs[2 * o][k] = acc[place, :, cut]
        for k, place in enumerate(places(bits, 1)):
            outs[2 * o + 1][k] = acc[place, :, cut].astype(BF16)


def tile_call(kernel, scalars, pieces, extra, tiles, shapes, scratch, cost):
    users = scalars[0].shape[0]
    tile_size = tiles.shape[1]
    count = len(pieces) * pieces[0][0].shape[1] // tile_size
    depth = sum(block.shape[0] for block in pieces[0])
    pieces = [block for blocks in pieces for block in blocks]
    smem = pl.BlockSpec(memory_space=pltpu.SMEM)
    vmem = pl.BlockSpec(memory_space=pltpu.VMEM)
    slab = jax.ShapeDtypeStruct((count, depth, tile_size), BF16)
    buf = jax.ShapeDtypeStruct((SLOTS, tile_size, tile_size), BF16)
    held = sum(x.size * x.dtype.itemsize for x in (*pieces, *extra, *shapes, *scratch, slab, buf))
    return pl.pallas_call(
        kernel,
        out_shape=shapes,
        in_specs=[smem] * len(scalars)
        + [vmem] * (len(pieces) + len(extra))
        + [pl.BlockSpec(memory_space=pl.ANY)],
        out_specs=[vmem] * len(shapes),
        scratch_shapes=[
            pltpu.VMEM(slab.shape, BF16),
            pltpu.VMEM(buf.shape, BF16),
            pltpu.SemaphoreType.DMA((SLOTS,)),
            pltpu.SMEM((users,), jnp.int32),
        ]
        + [pltpu.VMEM(x.shape, x.dtype) for x in scratch],
        compiler_params=pltpu.CompilerParams(vmem_limit_bytes=held + SPARE),
        cost_estimate=pl.CostEstimate(flops=0, bytes_accessed=cost, transcendentals=0),
    )(*scalars, *pieces, *extra, tiles)


def near_sums(scalars, pieces, tiles, rows):
    tile_size = tiles.shape[1]
    shapes = [jax.ShapeDtypeStruct((rows, kc, tile_size), F32) for kc in CHUNKS]
    return tile_call(
        functools.partial(near_kernel, len(pieces), len(pieces[0])), scalars, pieces, [], tiles, shapes, [], NEAR_COST
    )


def far_sums(scalars, pieces, start, tiles, orders, cost):
    rows, kc, tile_size = start.shape
    width = tile_size // len(orders)
    shapes = []
    for _ in orders:
        shapes.append(jax.ShapeDtypeStruct((rows // 2, kc, width), F32))
        shapes.append(jax.ShapeDtypeStruct((rows // 2, kc, width), BF16))
    return tile_call(
        functools.partial(far_kernel, len(pieces), len(pieces[0]), orders),
        scalars,
        pieces,
        [start],
        tiles,
        shapes,
        [jax.ShapeDtypeStruct(start.shape, F32)],
        cost,
    )


def mm(a, b):
    return lax.dot_general(a, b, (((1,), (0,)), ((), ())), precision=HIGH, preferred_element_type=F32)


def mmt(a, b):
    return lax.dot_general(a, b, (((1,), (1,)), ((), ())), precision=HIGH, preferred_element_type=F32)


def factor_kernel(packed, inverse, good):
    n = packed.shape[1]
    r = lax.broadcasted_iota(jnp.int32, (n, n), 0)
    c = lax.broadcasted_iota(jnp.int32, (n, n), 1)
    mixed = packed[:n]
    flipped = mixed.T
    side = packed[n : 2 * n]
    tail = jnp.broadcast_to(packed[2 * n : 2 * n + 1], (n, n))
    first = jnp.where(r >= c, mixed, flipped)
    second = jnp.where(r < c, mixed, jnp.where(r > c, flipped, tail))
    gram = jnp.concatenate(
        [jnp.concatenate([first, side.T], axis=1), jnp.concatenate([side, second], axis=1)], axis=0
    )
    m = 2 * n
    rr = lax.broadcasted_iota(jnp.int32, (m, m), 0)
    cc = lax.broadcasted_iota(jnp.int32, (m, m), 1)
    on = rr == cc
    eye = jnp.where(on, 1.0, 0.0).astype(F32)
    low = jnp.where(rr > cc, 1.0, jnp.where(on, 0.5, 0.0)).astype(F32)
    diag = jnp.where(on, gram, 0.0)
    scale_row = lax.rsqrt(jnp.sum(diag, axis=0, keepdims=True))
    scale_col = lax.rsqrt(jnp.sum(diag, axis=1, keepdims=True))
    unit = gram * scale_row * scale_col
    off = unit - eye
    square = jnp.dot(off, off, preferred_element_type=F32)
    spread = jnp.max(jnp.sum(jnp.abs(jnp.dot(square, square, preferred_element_type=F32)), axis=1))
    w = eye - low * off
    for _ in range(NEWTON):
        err = mmt(mm(w, unit), w) - eye
        w = w - mm(low * err, w)
    last = jnp.max(jnp.sum(jnp.abs(err), axis=1))
    inflation = jnp.max(jnp.sum(w * w, axis=0))
    inverse[...] = w * scale_row
    good[0] = jnp.where((spread < 0.025) & (last < 0.01) & (inflation < 1.1), 1, 0)


def factor(packed):
    n = packed.shape[1]
    return pl.pallas_call(
        factor_kernel,
        out_shape=[jax.ShapeDtypeStruct((2 * n, 2 * n), F32), jax.ShapeDtypeStruct((1,), jnp.int32)],
        in_specs=[pl.BlockSpec(memory_space=pltpu.VMEM)],
        out_specs=[pl.BlockSpec(memory_space=pltpu.VMEM), pl.BlockSpec(memory_space=pltpu.SMEM)],
        compiler_params=pltpu.CompilerParams(vmem_limit_bytes=24 * 2**20),
        cost_estimate=pl.CostEstimate(
            flops=0, bytes_accessed=FACTOR_COST, transcendentals=0
        ),
    )(packed)


def last_kernel(inverse, early, keep0, keep1, came, out):
    left = keep0[0] + came[0].astype(F32)
    right = keep1[0] + came[1].astype(F32)
    total = jnp.concatenate([early[...], jnp.concatenate([left, right], axis=1)], axis=0)
    w = inverse[...]
    wh, th = w.astype(BF16), total.astype(BF16)
    wl = (w - wh.astype(F32)).astype(BF16)
    tl = (total - th.astype(F32)).astype(BF16)
    small = jnp.dot(wh, tl, preferred_element_type=F32) + jnp.dot(wl, th, preferred_element_type=F32)
    out[...] = jnp.dot(wh, th, preferred_element_type=F32) + small


def last(inverse, early, keeps, came):
    vmem = pl.BlockSpec(memory_space=pltpu.VMEM)
    return pl.pallas_call(
        last_kernel,
        out_shape=jax.ShapeDtypeStruct((inverse.shape[0], early.shape[1]), F32),
        in_specs=[vmem] * 5,
        out_specs=vmem,
        compiler_params=pltpu.CompilerParams(vmem_limit_bytes=16 * 2**20),
    )(inverse, early, *keeps, came)


def full_path(rows, cols, sketch, tiles, tile_user, tile_item, tile_count, item_owner, packed):
    n = packed.shape[1]
    r = lax.broadcasted_iota(jnp.int32, (n, n), 0)
    c = lax.broadcasted_iota(jnp.int32, (n, n), 1)
    mixed, side, tail = packed[:n], packed[n : 2 * n], packed[2 * n : 2 * n + 1]
    first = jnp.where(r >= c, mixed, mixed.T)
    second = jnp.where(r < c, mixed, jnp.where(r > c, mixed.T, tail))
    gram = jnp.block([[first, side.T], [side, second]])
    lower = jnp.linalg.cholesky(gram)
    basis = lax.linalg.triangular_solve(lower, sketch, left_side=False, lower=True, transpose_a=True).astype(BF16)
    have = {0: basis}
    for bit in bits_of(cols):
        for place in list(have):
            have[place | bit] = swap(have[place], "cols", cols, bit)
    slab = jnp.concatenate([have[i] for i in range(cols)], axis=0)
    col = lax.axis_index("cols")
    row = lax.axis_index("rows")
    per_piece = sketch.shape[0] // tiles.shape[2]
    owner = item_owner[0]
    tile_size = tiles.shape[2]

    def step(index, sums):
        user = tile_user[index]
        block = lax.bitwise_xor(user // per_piece, col) * per_piece + user % per_piece
        part_rows = lax.dynamic_slice_in_dim(slab, block * tile_size, tile_size, 0)
        part = lax.dot_general(part_rows, tiles[index], (((0,), (0,)), ((), ())), preferred_element_type=F32)
        place = lax.bitwise_xor(owner[tile_item[index]], row)
        now = lax.dynamic_index_in_dim(sums, place, 0, keepdims=False)
        return lax.dynamic_update_index_in_dim(sums, now + part, place, 0)

    totals = jnp.zeros((owner.shape[0], sketch.shape[1], tile_size), F32)
    totals = lax.fori_loop(0, tile_count[0], step, totals)
    for bit in bits_of(rows):
        totals = totals[:bit] + swap(totals[bit:], "rows", rows, bit)
    return totals[0]


def after(value, *others):
    return lax.optimization_barrier((value, *others))[0]


def exchange(lanes, rows):
    groups = []
    for bit in sorted({lane[2] for lane in lanes}):
        members = [i for i, lane in enumerate(lanes) if lane[2] == bit]
        sent = [lanes[i][1].reshape(-1, lanes[i][1].shape[2]) for i in members]
        groups.append((members, swap(jnp.concatenate(sent, axis=0), "rows", rows, 1 << bit)))
    return groups


def received(lanes, groups):
    got = [None] * len(lanes)
    for members, came in groups:
        first = 0
        for i in members:
            shape = lanes[i][1].shape
            size = shape[0] * shape[1]
            got[i] = came[first : first + size].reshape(shape)
            first += size
    return [lane[0] + g.astype(F32) for lane, g in zip(lanes, got)]


def split(total):
    half = total.shape[0] // 2
    return total[:half], total[half:].astype(BF16)


def body(rows, cols, sketch, tiles, tile_user, tile_item, tile_count, item_owner):
    row_bits = rows.bit_length() - 1
    first_order = tuple(range(row_bits))
    orders = (first_order, (1, 0) + first_order[2:])
    row = lax.axis_index("rows")
    col = lax.axis_index("cols")
    meta = jnp.stack([tile_count[0], row, col]).astype(jnp.int32)
    scalars = (tile_user, tile_item, item_owner[0], meta)
    far_bit, *near_bits = bits_of(cols)

    def spread(piece):
        have = {0: piece}
        for bit in near_bits:
            for place in list(have):
                have[place | bit] = swap(have[place], "cols", cols, bit)
        return [have[i] for i in range(cols // 2)]

    fence = lax.optimization_barrier
    far = far_bit
    flat, *chunks = split_sketch(sketch)
    near = list(zip(*[spread(c) for c in chunks]))
    crossed = [swap(c, "cols", cols, far) for c in chunks]
    packed = packed_gram(flat)
    for bit in near_bits:
        packed = packed + swap(packed, "cols", cols, bit)
    came = swap(packed, "rows", rows, 2)
    near[0] = (after(near[0][0], packed), *near[0][1:])
    sums = near_sums(scalars, near, tiles, rows)
    packed, came, *sums = fence((packed, came, *sums))
    packed = packed + came
    came = swap(packed, "rows", rows, 4)
    crossed[0] = after(crossed[0], packed)
    outs = far_sums(scalars, [[p] for p in spread(crossed[0])], sums[0], tiles, orders, EARLY_COST)
    packed, came, *outs = fence((packed, came, *outs))
    packed = packed + came
    came = swap(packed, "cols", cols, far)
    lanes = [(outs[2 * o], outs[2 * o + 1], order[0]) for o, order in enumerate(orders)]
    groups = exchange(lanes, rows)
    crossed[1] = after(crossed[1], packed)
    later = far_sums(scalars, [[p] for p in spread(crossed[1])], sums[1], tiles, orders, LATE_COST)
    flying = [g[1] for g in groups]
    packed, came, *rest = fence((packed, came, *flying, *later))
    groups = [(g[0], x) for g, x in zip(groups, rest)]
    later = rest[len(groups) :]
    packed = packed + came
    stages = [1] + [1 << b for b in range(3, row_bits)]

    totals = received(lanes, groups)
    late = [(later[2 * o], later[2 * o + 1]) for o in range(len(orders))]
    for step in range(1, row_bits + 1):
        lanes = []
        if step < row_bits:
            lanes += [(*split(t), order[step]) for t, order in zip(totals, orders)]
        lanes += [(*pair, order[step - 1]) for pair, order in zip(late, orders)]
        groups = exchange(lanes, rows)
        flying = [g[1] for g in groups]
        sends = [lane[1] for lane in lanes]
        if step > 1 and step <= len(stages) + 1:
            packed = packed + after(came, *sends)
        if step <= len(stages):
            came = swap(packed, "rows", rows, stages[step - 1])
        if step == len(stages) + 1:
            inverse, good = factor(after(packed, *sends))
            free = [i for i, g in enumerate(groups) if max(g[0]) < len(lanes) - len(orders)]
            inverse, *tied = fence((inverse, *[flying[i] for i in free]))
            for i, x in zip(free, tied):
                flying[i] = x
        groups = [(g[0], x) for g, x in zip(groups, flying)]
        if step < row_bits:
            new = received(lanes, groups)
            totals, new = new[: len(orders)], new[len(orders) :]
            late = [split(t) for t in new]
        if step == row_bits - 1:
            early = jnp.concatenate([t[0] for t in totals], axis=1)
    keeps = [lane[0] for lane in lanes]
    came = groups[0][1].reshape(len(lanes), *lanes[0][1].shape[1:])
    out = lax.cond(
        good[0] > 0,
        lambda: last(inverse, early, keeps, came),
        lambda: full_path(rows, cols, flat.T, tiles, tile_user, tile_item, tile_count, item_owner, packed),
    )
    return out[None, None]


def solution(mesh):
    placed = (
        P(("rows", "cols"), None),
        P(("rows", "cols"), None, None),
        P(("rows", "cols")),
        P(("rows", "cols")),
        P(("rows", "cols")),
        P("cols", None),
    )
    return jax.shard_map(
        functools.partial(body, mesh.shape["rows"], mesh.shape["cols"]),
        mesh=mesh,
        in_specs=placed,
        out_specs=P("rows", "cols", None, None),
        check_vma=False,
    )
```

profile of v0, /device:TPU:2, one launch (start us, length us, event | category | flops | bytes accessed | tf_op | source)
XLA Modules:
  0.0 671.1 jit_solution(18339879074019053816)
XLA Ops:
  2.2 1.4 shard_map.67
  5.1 1.9 collective-permute-start.7
  7.7 4.8 shard_map.68
  12.5 6.3 collective-permute-done.11.refs_0_
  19.1 3.7 collective-permute-start.10
  22.8 4.1 shard_map.69
  26.9 2.4 collective-permute-done.10
  30.4 1.5 collective-permute-start.14
  31.9 2.2 collective-permute-start.15
  34.1 3.6 shard_map.70
  37.7 1.8 collective-permute-done.13
  40.5 1.7 collective-permute-done.15
  42.8 1.8 collective-permute-start.19
  44.6 1.8 collective-permute-start.18
  46.4 7.4 %collective-permute-done.20 = bf16[704,256]{1,0:T(8,128)(2,1)S(1)} collective-permute-done((bf16[704,256]{1,0:T(8,128)(2,1)S(1)}, bf16[704,256]{1,0:T(8,128)(2,1)S(1)}, u32[]{:S(2)}, u32[]{:S(2)}) %collective-permute-start.20) | collective-permute-done | bytes 360480 | tf_op jit(solution)/shard_map/ppermute | solution.py:29
  55.4 1.5 collective-permute-start.21
  57.5 2.1 collective-permute-start.24
  59.6 3.8 shard_map.71
  65.1 2.5 collective-permute-done.24
  67.7 3.0 collective-permute-done.23
  70.7 599.6 %conditional.1 = (f32[1,1,256,512]{3,2,1,0:T(8,128)S(1)}) conditional(s32[]{:T(128)} %bitcast.36, (s32[1]{0:T(128)}, f32[264,128]{1,0:T(8,128)S(1)}, f32[256,1024]{1,0:T(8,128)S(1)}, s32[1,8]{1,0:T(1,128)S(1)}, s32[40]{0:T(128)S(1)}, /*index=5*/s32[40]{0:T(128)S(1)}, bf16[40,512,512]{2,1,0:T(8,128)(2,1)}) %tuple.91, (f32[2,96,256]{2,1,0:T(8,128)S(1)}, ...), branch_computations={%region_0.7_spmd, %region_7.8_spmd} | conditional | flops 802537728 | bytes 80229168 | solution.py:489
  71.4 11.7 %cholesky.8 = f32[128,128]{1,0:T(8,128)S(1)} custom-call(f32[128,128]{1,0:T(8,128)S(1)} %cholesky.47), custom_call_target="Cholesky" | custom-call | tf_op jit(solution)/shard_map/cond/branch_0_fun/jit(cholesky)/cholesky | solution.py:354
  83.4 9.8 %custom-call.12 = f32[1,128,128]{1,2,0:T(8,128)S(1)} custom-call(f32[1,128,128]{2,1,0:T(8,128)S(1)} %copy.15), custom_call_target="InvertDiagBlocksLowerTriangular" | custom-call | tf_op jit(solution)/shard_map/cond/branch_0_fun/jit(cholesky)/cholesky | solution.py:354
  93.8 11.7 %cholesky.30 = f32[128,128]{1,0:T(8,128)S(1)} custom-call(f32[128,128]{1,0:T(8,128)S(1)} %convolution_subtract_fusion.1), custom_call_target="Cholesky" | custom-call | tf_op jit(solution)/shard_map/cond/branch_0_fun/jit(cholesky)/cholesky | solution.py:354
  107.7 4.1 while.13
  108.5 1.3 bitcast_dynamic-update-slice_fusion.2
  111.8 19.7 %custom-call.13 = f32[2,128,128]{1,2,0:T(8,128)S(1)} custom-call(f32[2,128,128]{2,1,0:T(8,128)S(1)} %get-tuple-element.267), custom_call_target="InvertDiagBlocksLowerTriangular" | custom-call | tf_op jit(solution)/shard_map/cond/branch_0_fun/triangular_solve | solution.py:355
  134.1 10.4 %collective-permute-done.1 = bf16[1024,256]{0,1:T(8,128)(2,1)S(1)} collective-permute-done((bf16[1024,256]{0,1:T(8,128)(2,1)S(1)}, bf16[1024,256]{0,1:T(8,128)(2,1)S(1)}, u32[]{:S(2)}, u32[]{:S(2)}) %collective-permute-start.1) | collective-permute-done | bytes 524320 | tf_op jit(solution)/shard_map/cond/branch_0_fun/ppermute | solution.py:29
  146.6 3.1 pad_maximum_fusion
  149.7 2.5 broadcast.96
  152.2 131.4 %while.12 = (s32[]{:T(128)}, f32[8,256,512]{2,1,0:T(8,128)}, s32[]{:T(128)}, s32[40]{0:T(128)S(1)}, s32[8]{0:T(128)S(1)}, /*index=5*/s32[]{:T(128)}, s32[40]{0:T...) while((s32[]{:T(128)}, f32[8,256,512]{2,1,0:T(8,128)}, ...), condition=%wide.region_6.6_spmd, body=%wide.region_5.5_spmd.sunk | while | flops 134348832 | bytes 2884192 | solution.py:377
  160.9 2.2 fusion.30
  171.8 2.2 fusion.30
  182.7 2.1 fusion.30
  193.6 2.2 fusion.30
  204.5 2.1 fusion.30
  215.4 2.2 fusion.30
  226.3 2.2 fusion.30
  237.2 2.2 fusion.30
  248.1 2.2 fusion.30
  259.0 2.1 fusion.30
  269.9 2.2 fusion.30
  280.8 2.2 fusion.30
  283.6 1.9 slice.118
  285.6 304.7 %collective-permute-start.3 = (f32[4,256,512]{2,1,0:T(8,128)S(1)}, f32[4,256,512]{2,1,0:T(8,128)S(1)}, u32[]{:S(2)}, u32[]{:S(2)}) collective-permute-start(f32[4,256,512]{2,1,0:T(8,128)S(1)} %slice.118), channel_id=1, source_target_pairs={{0,16},{4,20},{8,24},{12,28},{16,0},{20,4},{24,8},{28,12},{1,17},{... | collective-permute-start | bytes 6291464 | tf_op jit(solution)/shard_map/cond/branch_0_fun/ppermute | solution.py:29
  590.3 46.5 %collective-permute-done.3 = f32[4,256,512]{2,1,0:T(8,128)S(1)} collective-permute-done((f32[4,256,512]{2,1,0:T(8,128)S(1)}, f32[4,256,512]{2,1,0:T(8,128)S(1)}, u32[]{:S(2)}, u32[]{:S(2)}) %collective-permute-start.3) | collective-permute-done | bytes 2097184 | tf_op jit(solution)/shard_map/cond/branch_0_fun/ppermute | solution.py:29
  637.4 21.8 %collective-permute-done.4 = f32[2,256,512]{2,1,0:T(8,128)S(1)} collective-permute-done((f32[2,256,512]{2,1,0:T(8,128)S(1)}, f32[2,256,512]{2,1,0:T(8,128)S(1)}, u32[]{:S(2)}, u32[]{:S(2)}) %collective-permute-start.4) | collective-permute-done | bytes 1048608 | tf_op jit(solution)/shard_map/cond/branch_0_fun/ppermute | solution.py:29
  659.6 10.4 %collective-permute-done.5 = f32[1,256,512]{2,1,0:T(8,128)S(1)} collective-permute-done((f32[1,256,512]{2,1,0:T(8,128)S(1)}, f32[1,256,512]{2,1,0:T(8,128)S(1)}, u32[]{:S(2)}, u32[]{:S(2)}) %collective-permute-start.5) | collective-permute-done | bytes 524320 | tf_op jit(solution)/shard_map/cond/branch_0_fun/ppermute | solution.py:29
  (167 shorter events, 55.4 us)
Async XLA Ops:
  0.0 1.2 copy-start
  1.6 3.5 copy-start.2
  1.6 6.1 collective-permute-start.8
  1.7 17.1 %collective-permute-start.11 = (bf16[320,1024]{1,0:T(8,128)(2,1)S(1)}, bf16[320,1024]{1,0:T(8,128)(2,1)S(1)}, u32[]{:S(2)}, u32[]{:S(2)}) collective-permute-start(bf16[320,1024]{1,0:T(8,128)(2,1)S(1)} %get-tuple-element.221.refs_0_), channel_id=1, source_target_pairs={{0,2},{1,3},{2,0},{3,1},{4,6},{5,7},{6,4},{7,5},{8,10},{9,11},{10,... | collective-permute-start | bytes 1966088 | tf_op jit(solution)/shard_map/ppermute | solution.py:29
  1.8 5.9 collective-permute-start.9
  3.6 1.4 collective-permute-start.6
  5.1 7.5 %collective-permute-start.7 = (f32[264,128]{1,0:T(8,128)S(1)}, f32[264,128]{1,0:T(8,128)S(1)}, u32[]{:S(2)}, u32[]{:S(2)}) collective-permute-start(f32[264,128]{1,0:T(8,128)S(1)} %add.134), channel_id=1, source_target_pairs={{0,8},{4,12},{8,0},{12,4},{16,24},{20,28},{24,16},{28,20},{1,9},{5... | collective-permute-start | bytes 405512 | tf_op jit(solution)/shard_map/ppermute | solution.py:29
  7.7 15.1 %copy-start.6 = (s32[1,8]{1,0:T(1,128)S(1)}, s32[1,8]{1,0:T(1,128)}, u32[]{:S(2)}) copy-start(s32[1,8]{1,0:T(1,128)} %param.15) | copy-start | bytes 100
  7.7 15.1 %copy-start.7 = (s32[40]{0:T(128)S(1)}, s32[40]{0:T(128)}, u32[]{:S(2)}) copy-start(s32[40]{0:T(128)} %items.5) | copy-start | bytes 484
  7.7 15.1 %copy-start.8 = (s32[40]{0:T(128)S(1)}, s32[40]{0:T(128)}, u32[]{:S(2)}) copy-start(s32[40]{0:T(128)} %users.5) | copy-start | bytes 484
  18.8 4.0 collective-permute-start.12
  18.8 11.5 %collective-permute-start.16 = (bf16[192,1024]{1,0:T(8,128)(2,1)S(1)}, bf16[192,1024]{1,0:T(8,128)(2,1)S(1)}, u32[]{:S(2)}, u32[]{:S(2)}) collective-permute-start(bf16[192,1024]{1,0:T(8,128)(2,1)S(1)} %get-tuple-element.222.refs_1_), channel_id=1, source_target_pairs={{0,2},{1,3},{2,0},{3,1},{4,6},{5,7},{6,4},{7,5},{8,10},{9,11},{10,... | collective-permute-start | bytes 1179656 | tf_op jit(solution)/shard_map/ppermute | solution.py:29
  19.1 10.1 %collective-permute-start.10 = (f32[264,128]{1,0:T(8,128)S(1)}, f32[264,128]{1,0:T(8,128)S(1)}, u32[]{:S(2)}, u32[]{:S(2)}) collective-permute-start(f32[264,128]{1,0:T(8,128)S(1)} %add.135), channel_id=1, source_target_pairs={{0,16},{4,20},{8,24},{12,28},{16,0},{20,4},{24,8},{28,12},{1,17},{... | collective-permute-start | bytes 405512 | tf_op jit(solution)/shard_map/ppermute | solution.py:29
  30.4 3.8 collective-permute-start.17
  30.4 10.1 %collective-permute-start.14 = (bf16[640,256]{1,0:T(8,128)(2,1)S(1)}, bf16[640,256]{1,0:T(8,128)(2,1)S(1)}, u32[]{:S(2)}, u32[]{:S(2)}) collective-permute-start(bf16[640,256]{1,0:T(8,128)(2,1)S(1)} %bitcast.122), channel_id=1, source_target_pairs={{0,4},{4,0},{8,12},{12,8},{16,20},{20,16},{24,28},{28,24},{1,5},{5... | collective-permute-start | bytes 983048 | tf_op jit(solution)/shard_map/ppermute | solution.py:29
  31.9 10.3 %collective-permute-start.15 = (bf16[640,256]{1,0:T(8,128)(2,1)S(1)}, bf16[640,256]{1,0:T(8,128)(2,1)S(1)}, u32[]{:S(2)}, u32[]{:S(2)}) collective-permute-start(bf16[640,256]{1,0:T(8,128)(2,1)S(1)} %bitcast.121), channel_id=1, source_target_pairs={{0,8},{4,12},{8,0},{12,4},{16,24},{20,28},{24,16},{28,20},{1,9},{5... | collective-permute-start | bytes 983048 | tf_op jit(solution)/shard_map/ppermute | solution.py:29
  34.1 5.4 collective-permute-start.13
  42.4 11.4 %collective-permute-start.20 = (bf16[704,256]{1,0:T(8,128)(2,1)S(1)}, bf16[704,256]{1,0:T(8,128)(2,1)S(1)}, u32[]{:S(2)}, u32[]{:S(2)}) collective-permute-start(bf16[704,256]{1,0:T(8,128)(2,1)S(1)} %pad_maximum_fusion.3), channel_id=1, source_target_pairs={{0,4},{4,0},{8,12},{12,8},{16,20},{20,16},{24,28},{28,24},{1,5},{5... | collective-permute-start | bytes 1081352 | tf_op jit(solution)/shard_map/ppermute | solution.py:29
  42.8 11.0 %collective-permute-start.19 = (bf16[704,256]{1,0:T(8,128)(2,1)S(1)}, bf16[704,256]{1,0:T(8,128)(2,1)S(1)}, u32[]{:S(2)}, u32[]{:S(2)}) collective-permute-start(bf16[704,256]{1,0:T(8,128)(2,1)S(1)} %pad_maximum_fusion.2), channel_id=1, source_target_pairs={{0,8},{4,12},{8,0},{12,4},{16,24},{20,28},{24,16},{28,20},{1,9},{5... | collective-permute-start | bytes 1081352 | tf_op jit(solution)/shard_map/ppermute | solution.py:29
  44.6 10.7 %collective-permute-start.18 = (f32[264,128]{1,0:T(8,128)S(1)}, f32[264,128]{1,0:T(8,128)S(1)}, u32[]{:S(2)}, u32[]{:S(2)}) collective-permute-start(f32[264,128]{1,0:T(8,128)S(1)} %add.137), channel_id=1, source_target_pairs={{0,4},{4,0},{8,12},{12,8},{16,20},{20,16},{24,28},{28,24},{1,5},{5... | collective-permute-start | bytes 405512 | tf_op jit(solution)/shard_map/ppermute | solution.py:29
  53.9 16.9 %copy-start.3 = (f32[256,1024]{1,0:T(8,128)S(1)}, f32[256,1024]{1,0:T(8,128)}, u32[]{:S(2)}) copy-start(f32[256,1024]{1,0:T(8,128)} %copy-done.2) | copy-start | bytes 3145732
  55.4 8.7 %collective-permute-start.21 = (bf16[192,256]{1,0:T(8,128)(2,1)S(1)}, bf16[192,256]{1,0:T(8,128)(2,1)S(1)}, u32[]{:S(2)}, u32[]{:S(2)}) collective-permute-start(bf16[192,256]{1,0:T(8,128)(2,1)S(1)} %bitcast.134), channel_id=1, source_target_pairs={{0,8},{4,12},{8,0},{12,4},{16,24},{20,28},{24,16},{28,20},{1,9},{5... | collective-permute-start | bytes 294920 | tf_op jit(solution)/shard_map/ppermute | solution.py:29
  56.9 7.3 %collective-permute-start.22 = (bf16[192,256]{1,0:T(8,128)(2,1)S(1)}, bf16[192,256]{1,0:T(8,128)(2,1)S(1)}, u32[]{:S(2)}, u32[]{:S(2)}) collective-permute-start(bf16[192,256]{1,0:T(8,128)(2,1)S(1)} %bitcast.135), channel_id=1, source_target_pairs={{0,4},{4,0},{8,12},{12,8},{16,20},{20,16},{24,28},{28,24},{1,5},{5... | collective-permute-start | bytes 294920 | tf_op jit(solution)/shard_map/ppermute | solution.py:29
  57.5 10.1 %collective-permute-start.24 = (bf16[320,256]{1,0:T(8,128)(2,1)S(1)}, bf16[320,256]{1,0:T(8,128)(2,1)S(1)}, u32[]{:S(2)}, u32[]{:S(2)}) collective-permute-start(bf16[320,256]{1,0:T(8,128)(2,1)S(1)} %pad_maximum_fusion.5), channel_id=1, source_target_pairs={{0,16},{4,20},{8,24},{12,28},{16,0},{20,4},{24,8},{28,12},{1,17},{... | collective-permute-start | bytes 491528 | tf_op jit(solution)/shard_map/ppermute | solution.py:29
  64.2 6.5 collective-permute-start.23
  133.4 11.2 %collective-permute-start.1 = (bf16[1024,256]{0,1:T(8,128)(2,1)S(1)}, bf16[1024,256]{0,1:T(8,128)(2,1)S(1)}, u32[]{:S(2)}, u32[]{:S(2)}) collective-permute-start(bf16[1024,256]{0,1:T(8,128)(2,1)S(1)} %pad_maximum_fusion.1), channel_id=1, source_target_pairs={{0,2},{1,3},{2,0},{3,1},{4,6},{5,7},{6,4},{7,5},{8,10},{9,11},{10,... | collective-permute-start | bytes 1572872 | tf_op jit(solution)/shard_map/cond/branch_0_fun/ppermute | solution.py:29
  134.1 10.5 %collective-permute-start = (bf16[1024,256]{0,1:T(8,128)(2,1)S(1)}, bf16[1024,256]{0,1:T(8,128)(2,1)S(1)}, u32[]{:S(2)}, u32[]{:S(2)}) collective-permute-start(bf16[1024,256]{0,1:T(8,128)(2,1)S(1)} %pad_maximum_fusion.1), channel_id=1, source_target_pairs={{0,1},{1,0},{2,3},{3,2},{4,5},{5,4},{6,7},{7,6},{8,9},{9,8},{10,11... | collective-permute-start | bytes 1572872 | tf_op jit(solution)/shard_map/cond/branch_0_fun/ppermute | solution.py:29
  144.6 2.0 collective-permute-start.2
  144.6 0.8 copy-start.5
  283.6 353.2 %copy-start.1 = (f32[8,256,512]{2,1,0:T(8,128)S(1)}, f32[8,256,512]{2,1,0:T(8,128)}, u32[]{:S(2)}) copy-start(f32[8,256,512]{2,1,0:T(8,128)} %get-tuple-element.173) | copy-start | bytes 12582916 | tf_op jit(solution)/shard_map/cond
  285.6 351.2 %collective-permute-start.3 = (f32[4,256,512]{2,1,0:T(8,128)S(1)}, f32[4,256,512]{2,1,0:T(8,128)S(1)}, u32[]{:S(2)}, u32[]{:S(2)}) collective-permute-start(f32[4,256,512]{2,1,0:T(8,128)S(1)} %slice.118), channel_id=1, source_target_pairs={{0,16},{4,20},{8,24},{12,28},{16,0},{20,4},{24,8},{28,12},{1,17},{... | collective-permute-start | bytes 6291464 | tf_op jit(solution)/shard_map/cond/branch_0_fun/ppermute | solution.py:29
  637.3 21.9 %collective-permute-start.4 = (f32[2,256,512]{2,1,0:T(8,128)S(1)}, f32[2,256,512]{2,1,0:T(8,128)S(1)}, u32[]{:S(2)}, u32[]{:S(2)}) collective-permute-start(f32[2,256,512]{2,1,0:T(8,128)S(1)} %slice.178), channel_id=1, source_target_pairs={{0,8},{4,12},{8,0},{12,4},{16,24},{20,28},{24,16},{28,20},{1,9},{5... | collective-permute-start | bytes 3145736 | tf_op jit(solution)/shard_map/cond/branch_0_fun/ppermute | solution.py:29
  659.5 10.5 %collective-permute-start.5 = (f32[1,256,512]{2,1,0:T(8,128)S(1)}, f32[1,256,512]{2,1,0:T(8,128)S(1)}, u32[]{:S(2)}, u32[]{:S(2)}) collective-permute-start(f32[1,256,512]{2,1,0:T(8,128)S(1)} %slice.180), channel_id=1, source_target_pairs={{0,4},{4,0},{8,12},{12,8},{16,20},{20,16},{24,28},{28,24},{1,5},{5... | collective-permute-start | bytes 1572872 | tf_op jit(solution)/shard_map/cond/branch_0_fun/ppermute | solution.py:29
  670.3 0.8 copy-start.4
where the time goes:
time: 683 us; the launch traced here: 671 us
  starting transfers between devices  325 us (48%)
  waiting for transfers between devices  120 us (18%)
  loops' own time  73.3 us (11%)
  other arithmetic  58.5 us (9%)
  local copies, waits for them, and re-layouts  46.4 us (7%)
  matrix products  28.2 us (4%)
  Pallas kernels  18 us (3%)
    ppermute x25, starting transfers between devices, swap(): return lax.ppermute(x, axis, [(i, i ^ bit) for i in range(count)])  325 us
    ppermute x25, waiting for transfers between devices, swap(): return lax.ppermute(x, axis, [(i, i ^ bit) for i in range(count)])  120 us
    another operation x1, loops' own time, full_path(): totals = lax.fori_loop(0, tile_count[0], step, totals)  71.4 us
    another operation x6, other arithmetic, full_path(): lower = jnp.linalg.cholesky(gram)  34.1 us
    dot_general x12, matrix products, step(): lax.dot_general(part_rows, tiles[index], (((0,), (0,)), ((), ())), prefer...  25.9 us
    another operation x5, other arithmetic, full_path(): lax.linalg.triangular_solve(lower, sketch, left_side=False, lower=True, t...  19.8 us
    dynamic_slice x24, local copies, waits for them, and re-layouts, step(): place = lax.bitwise_xor(owner[tile_item[index]], row)  14.1 us
  transfers between devices with their start and end apart: 25, of which 16 were waited for; matrix products, arithmetic and copies ran while one was open for 0% of the time, Pallas kernels for 3%

commit v1 on v0

--- a/solution.py
+++ b/solution.py
@@ -17,7 +17,7 @@
 EARLY_COST = 1024
 LATE_COST = 1024
 FACTOR_COST = 200 * 2**20
-CHUNKS = (160, 96)
+CHUNKS = (176, 80)
 NEWTON = 2
 
 

time: 683 us -> 678 us (level); the launches traced: 671 us -> 677 us
  starting transfers between devices: 325 us -> 391 us
  loops' own time: 73.3 us -> 38 us
  local copies, waits for them, and re-layouts: 46.4 us -> 29.3 us
  matrix products: 28.2 us -> 15.2 us
  waiting for transfers between devices: 120 us -> 128 us
    ppermute x25, starting transfers between devices: 325 us -> 391 us  [swap(): return lax.ppermute(x, axis, [(i, i ^ bit) for i in range(count)])]
    another operation x1, loops' own time: 71.4 us -> 36 us  [full_path(): totals = lax.fori_loop(0, tile_count[0], step, totals)]
    dot_general x12 -> x6, matrix products: 25.9 us -> 12.9 us  [step(): lax.dot_general(part_rows, tiles[index], (((0,), (0,)), ((), ())), prefer...]
    ppermute x25, waiting for transfers between devices: 120 us -> 128 us  [swap(): return lax.ppermute(x, axis, [(i, i ^ bit) for i in range(count)])]
    dynamic_slice x24 -> x12, local copies, waits for them, and re-layouts: 14.1 us -> 7.04 us  [step(): place = lax.bitwise_xor(owner[tile_item[index]], row)]
  transfers between devices with their start and end apart: 25 -> 25, of which waited for: 16 -> 18; matrix products, arithmetic and copies ran while one was open for 0% -> 0% of each run, Pallas kernels for 3% -> 2%
where the time goes in v1:
time: 678 us; the launch traced here: 677 us
  starting transfers between devices  391 us (58%)
  waiting for transfers between devices  128 us (19%)
  other arithmetic  58.5 us (9%)
  loops' own time  38 us (6%)
  local copies, waits for them, and re-layouts  29.3 us (4%)
  matrix products  15.2 us (2%)
  Pallas kernels  15 us (2%)
    ppermute x25, starting transfers between devices, swap(): return lax.ppermute(x, axis, [(i, i ^ bit) for i in range(count)])  391 us
    ppermute x25, waiting for transfers between devices, swap(): return lax.ppermute(x, axis, [(i, i ^ bit) for i in range(count)])  128 us
    another operation x1, loops' own time, full_path(): totals = lax.fori_loop(0, tile_count[0], step, totals)  36 us
    another operation x6, other arithmetic, full_path(): lower = jnp.linalg.cholesky(gram)  34.1 us
    another operation x5, other arithmetic, full_path(): lax.linalg.triangular_solve(lower, sketch, left_side=False, lower=True, t...  19.8 us
  transfers between devices with their start and end apart: 25, of which 18 were waited for; matrix products, arithmetic and copies ran while one was open for 0% of the time, Pallas kernels for 2%

profile of v1, /device:TPU:2, one launch (start us, length us, event | category | flops | bytes accessed | tf_op | source)
XLA Modules:
  0.0 677.0 jit_solution(6879032117542234280)
XLA Ops:
  0.0 1.2 copy-done
  2.2 1.4 shard_map.67
  3.8 1.2 collective-permute-done.6
  5.1 1.9 collective-permute-start.7
  7.7 2.5 shard_map.68
  11.1 9.2 %collective-permute-done.11.refs_0_ = bf16[352,1024]{1,0:T(8,128)(2,1)S(1)} collective-permute-done((bf16[352,1024]{1,0:T(8,128)(2,1)S(1)}, bf16[352,1024]{1,0:T(8,128)(2,1)S(1)}, u32[]{:S(2)}, u32[]{:S(2)}) %collective-permute-start.11) | collective-permute-done | bytes 720928 | tf_op jit(solution)/shard_map/ppermute | solution.py:29
  20.5 2.9 collective-permute-start.10
  23.4 3.7 shard_map.69
  27.1 3.1 collective-permute-done.10
  30.2 1.6 collective-permute-start.14
  31.8 2.0 collective-permute-start.15
  34.2 1.4 collective-permute-done.17.refs_1_
  35.6 3.1 shard_map.70
  38.7 1.2 collective-permute-done.13
  42.3 1.3 collective-permute-start.19
  43.7 1.4 collective-permute-start.18
  45.1 6.4 collective-permute-done.20
  53.2 1.6 collective-permute-start.22
  54.9 4.2 collective-permute-start.24
  59.1 3.8 shard_map.71
  63.7 4.4 collective-permute-done.24
  69.3 606.9 %conditional.1 = (f32[1,1,256,512]{3,2,1,0:T(8,128)S(1)}) conditional(s32[]{:T(128)} %bitcast.36, (s32[1]{0:T(128)}, f32[264,128]{1,0:T(8,128)S(1)}, f32[256,1024]{1,0:T(8,128)S(1)}, s32[1,8]{1,0:T(1,128)S(1)}, s32[40]{0:T(128)S(1)}, /*index=5*/s32[40]{0:T(128)S(1)}, bf16[40,512,512]{2,1,0:T(8,128)(2,1)}) %tuple.91, (f32[2,80,256]{2,1,0:T(8,128)S(1)}, ...), branch_computations={%region_0.7_spmd, %region_7.8_spmd} | conditional | flops 802537728 | bytes 80229168 | solution.py:489
  70.0 11.7 %cholesky.8 = f32[128,128]{1,0:T(8,128)S(1)} custom-call(f32[128,128]{1,0:T(8,128)S(1)} %cholesky.47), custom_call_target="Cholesky" | custom-call | tf_op jit(solution)/shard_map/cond/branch_0_fun/jit(cholesky)/cholesky | solution.py:354
  82.0 9.8 %custom-call.12 = f32[1,128,128]{1,2,0:T(8,128)S(1)} custom-call(f32[1,128,128]{2,1,0:T(8,128)S(1)} %copy.15), custom_call_target="InvertDiagBlocksLowerTriangular" | custom-call | tf_op jit(solution)/shard_map/cond/branch_0_fun/jit(cholesky)/cholesky | solution.py:354
  92.3 11.7 %cholesky.30 = f32[128,128]{1,0:T(8,128)S(1)} custom-call(f32[128,128]{1,0:T(8,128)S(1)} %convolution_subtract_fusion.1), custom_call_target="Cholesky" | custom-call | tf_op jit(solution)/shard_map/cond/branch_0_fun/jit(cholesky)/cholesky | solution.py:354
  106.3 4.1 while.13
  107.1 1.3 bitcast_dynamic-update-slice_fusion.2
  109.0 1.3 bitcast_dynamic-update-slice_fusion.2
  110.3 19.7 %custom-call.13 = f32[2,128,128]{1,2,0:T(8,128)S(1)} custom-call(f32[2,128,128]{2,1,0:T(8,128)S(1)} %get-tuple-element.267), custom_call_target="InvertDiagBlocksLowerTriangular" | custom-call | tf_op jit(solution)/shard_map/cond/branch_0_fun/triangular_solve | solution.py:355
  132.0 1.9 collective-permute-start.1
  133.8 11.4 %collective-permute-done.1 = bf16[1024,256]{0,1:T(8,128)(2,1)S(1)} collective-permute-done((bf16[1024,256]{0,1:T(8,128)(2,1)S(1)}, bf16[1024,256]{0,1:T(8,128)(2,1)S(1)}, u32[]{:S(2)}, u32[]{:S(2)}) %collective-permute-start.1) | collective-permute-done | bytes 524320 | tf_op jit(solution)/shard_map/cond/branch_0_fun/ppermute | solution.py:29
  146.0 1.2 collective-permute-done.2
  147.3 3.1 pad_maximum_fusion
  150.3 2.5 broadcast.96
  152.9 66.0 %while.12 = (s32[]{:T(128)}, f32[8,256,512]{2,1,0:T(8,128)}, s32[]{:T(128)}, s32[40]{0:T(128)S(1)}, s32[8]{0:T(128)S(1)}, /*index=5*/s32[]{:T(128)}, s32[40]{0:T...) while((s32[]{:T(128)}, f32[8,256,512]{2,1,0:T(8,128)}, ...), condition=%wide.region_6.6_spmd, body=%wide.region_5.5_spmd.sunk | while | flops 134348832 | bytes 2884192 | solution.py:377
  161.6 2.2 fusion.30
  172.5 2.2 fusion.30
  183.4 2.1 fusion.30
  193.2 1.1 constant_dynamic-slice_fusion.4
  194.3 2.1 fusion.30
  205.1 2.1 fusion.30
  216.0 2.2 fusion.30
  218.8 1.9 slice.118
  220.8 21.2 %collective-permute-start.3 = (f32[4,256,512]{2,1,0:T(8,128)S(1)}, f32[4,256,512]{2,1,0:T(8,128)S(1)}, u32[]{:S(2)}, u32[]{:S(2)}) collective-permute-start(f32[4,256,512]{2,1,0:T(8,128)S(1)} %slice.118), channel_id=1, source_target_pairs={{0,16},{4,20},{8,24},{12,28},{16,0},{20,4},{24,8},{28,12},{1,17},{... | collective-permute-start | bytes 6291464 | tf_op jit(solution)/shard_map/cond/branch_0_fun/ppermute | solution.py:29
  242.0 46.5 %collective-permute-done.3 = f32[4,256,512]{2,1,0:T(8,128)S(1)} collective-permute-done((f32[4,256,512]{2,1,0:T(8,128)S(1)}, f32[4,256,512]{2,1,0:T(8,128)S(1)}, u32[]{:S(2)}, u32[]{:S(2)}) %collective-permute-start.3) | collective-permute-done | bytes 2097184 | tf_op jit(solution)/shard_map/cond/branch_0_fun/ppermute | solution.py:29
  289.0 348.7 %collective-permute-start.4 = (f32[2,256,512]{2,1,0:T(8,128)S(1)}, f32[2,256,512]{2,1,0:T(8,128)S(1)}, u32[]{:S(2)}, u32[]{:S(2)}) collective-permute-start(f32[2,256,512]{2,1,0:T(8,128)S(1)} %slice.178), channel_id=1, source_target_pairs={{0,8},{4,12},{8,0},{12,4},{16,24},{20,28},{24,16},{28,20},{1,9},{5... | collective-permute-start | bytes 3145736 | tf_op jit(solution)/shard_map/cond/branch_0_fun/ppermute | solution.py:29
  637.7 23.9 %collective-permute-done.4 = f32[2,256,512]{2,1,0:T(8,128)S(1)} collective-permute-done((f32[2,256,512]{2,1,0:T(8,128)S(1)}, f32[2,256,512]{2,1,0:T(8,128)S(1)}, u32[]{:S(2)}, u32[]{:S(2)}) %collective-permute-start.4) | collective-permute-done | bytes 1048608 | tf_op jit(solution)/shard_map/cond/branch_0_fun/ppermute | solution.py:29
  661.9 13.9 %collective-permute-done.5 = f32[1,256,512]{2,1,0:T(8,128)S(1)} collective-permute-done((f32[1,256,512]{2,1,0:T(8,128)S(1)}, f32[1,256,512]{2,1,0:T(8,128)S(1)}, u32[]{:S(2)}, u32[]{:S(2)}) %collective-permute-start.5) | collective-permute-done | bytes 524320 | tf_op jit(solution)/shard_map/cond/branch_0_fun/ppermute | solution.py:29
  (137 shorter events, 32.0 us)
Async XLA Ops:
  0.0 1.2 copy-start
  1.6 3.5 copy-start.2
  1.6 6.1 collective-permute-start.8
  1.7 18.6 %collective-permute-start.11 = (bf16[352,1024]{1,0:T(8,128)(2,1)S(1)}, bf16[352,1024]{1,0:T(8,128)(2,1)S(1)}, u32[]{:S(2)}, u32[]{:S(2)}) collective-permute-start(bf16[352,1024]{1,0:T(8,128)(2,1)S(1)} %get-tuple-element.221.refs_0_), channel_id=1, source_target_pairs={{0,2},{1,3},{2,0},{3,1},{4,6},{5,7},{6,4},{7,5},{8,10},{9,11},{10,... | collective-permute-start | bytes 2162696 | tf_op jit(solution)/shard_map/ppermute | solution.py:29
  1.8 5.9 collective-permute-start.9
  3.6 1.4 collective-permute-start.6
  5.1 6.0 collective-permute-start.7
  7.7 15.7 %copy-start.6 = (s32[1,8]{1,0:T(1,128)S(1)}, s32[1,8]{1,0:T(1,128)}, u32[]{:S(2)}) copy-start(s32[1,8]{1,0:T(1,128)} %param.15) | copy-start | bytes 100
  7.7 15.7 %copy-start.7 = (s32[40]{0:T(128)S(1)}, s32[40]{0:T(128)}, u32[]{:S(2)}) copy-start(s32[40]{0:T(128)} %items.5) | copy-start | bytes 484
  7.7 15.7 %copy-start.8 = (s32[40]{0:T(128)S(1)}, s32[40]{0:T(128)}, u32[]{:S(2)}) copy-start(s32[40]{0:T(128)} %users.5) | copy-start | bytes 484
  20.2 3.1 collective-permute-start.12
  20.2 13.6 %collective-permute-start.16 = (bf16[160,1024]{1,0:T(8,128)(2,1)S(1)}, bf16[160,1024]{1,0:T(8,128)(2,1)S(1)}, u32[]{:S(2)}, u32[]{:S(2)}) collective-permute-start(bf16[160,1024]{1,0:T(8,128)(2,1)S(1)} %get-tuple-element.222.refs_1_), channel_id=1, source_target_pairs={{0,2},{1,3},{2,0},{3,1},{4,6},{5,7},{6,4},{7,5},{8,10},{9,11},{10,... | collective-permute-start | bytes 983048 | tf_op jit(solution)/shard_map/ppermute | solution.py:29
  20.5 9.7 %collective-permute-start.10 = (f32[264,128]{1,0:T(8,128)S(1)}, f32[264,128]{1,0:T(8,128)S(1)}, u32[]{:S(2)}, u32[]{:S(2)}) collective-permute-start(f32[264,128]{1,0:T(8,128)S(1)} %add.135), channel_id=1, source_target_pairs={{0,16},{4,20},{8,24},{12,28},{16,0},{20,4},{24,8},{28,12},{1,17},{... | collective-permute-start | bytes 405512 | tf_op jit(solution)/shard_map/ppermute | solution.py:29
  30.2 10.0 %collective-permute-start.14 = (bf16[704,256]{1,0:T(8,128)(2,1)S(1)}, bf16[704,256]{1,0:T(8,128)(2,1)S(1)}, u32[]{:S(2)}, u32[]{:S(2)}) collective-permute-start(bf16[704,256]{1,0:T(8,128)(2,1)S(1)} %bitcast.122), channel_id=1, source_target_pairs={{0,4},{4,0},{8,12},{12,8},{16,20},{20,16},{24,28},{28,24},{1,5},{5... | collective-permute-start | bytes 1081352 | tf_op jit(solution)/shard_map/ppermute | solution.py:29
  31.8 9.4 %collective-permute-start.15 = (bf16[704,256]{1,0:T(8,128)(2,1)S(1)}, bf16[704,256]{1,0:T(8,128)(2,1)S(1)}, u32[]{:S(2)}, u32[]{:S(2)}) collective-permute-start(bf16[704,256]{1,0:T(8,128)(2,1)S(1)} %bitcast.121), channel_id=1, source_target_pairs={{0,8},{4,12},{8,0},{12,4},{16,24},{20,28},{24,16},{28,20},{1,9},{5... | collective-permute-start | bytes 1081352 | tf_op jit(solution)/shard_map/ppermute | solution.py:29
  33.9 1.7 collective-permute-start.17
  34.0 6.0 collective-permute-start.13
  41.4 10.1 %collective-permute-start.20 = (bf16[672,256]{1,0:T(8,128)(2,1)S(1)}, bf16[672,256]{1,0:T(8,128)(2,1)S(1)}, u32[]{:S(2)}, u32[]{:S(2)}) collective-permute-start(bf16[672,256]{1,0:T(8,128)(2,1)S(1)} %pad_maximum_fusion.4), channel_id=1, source_target_pairs={{0,4},{4,0},{8,12},{12,8},{16,20},{20,16},{24,28},{28,24},{1,5},{5... | collective-permute-start | bytes 1032200 | tf_op jit(solution)/shard_map/ppermute | solution.py:29
  42.3 9.4 %collective-permute-start.19 = (bf16[672,256]{1,0:T(8,128)(2,1)S(1)}, bf16[672,256]{1,0:T(8,128)(2,1)S(1)}, u32[]{:S(2)}, u32[]{:S(2)}) collective-permute-start(bf16[672,256]{1,0:T(8,128)(2,1)S(1)} %pad_maximum_fusion.3), channel_id=1, source_target_pairs={{0,8},{4,12},{8,0},{12,4},{16,24},{20,28},{24,16},{28,20},{1,9},{5... | collective-permute-start | bytes 1032200 | tf_op jit(solution)/shard_map/ppermute | solution.py:29
  43.7 9.2 %collective-permute-start.18 = (f32[264,128]{1,0:T(8,128)S(1)}, f32[264,128]{1,0:T(8,128)S(1)}, u32[]{:S(2)}, u32[]{:S(2)}) collective-permute-start(f32[264,128]{1,0:T(8,128)S(1)} %add.137), channel_id=1, source_target_pairs={{0,4},{4,0},{8,12},{12,8},{16,20},{20,16},{24,28},{28,24},{1,5},{5... | collective-permute-start | bytes 405512 | tf_op jit(solution)/shard_map/ppermute | solution.py:29
  51.5 17.8 %copy-start.3 = (f32[256,1024]{1,0:T(8,128)S(1)}, f32[256,1024]{1,0:T(8,128)}, u32[]{:S(2)}) copy-start(f32[256,1024]{1,0:T(8,128)} %copy-done.2) | copy-start | bytes 3145732
  53.0 10.6 %collective-permute-start.21 = (bf16[160,256]{1,0:T(8,128)(2,1)S(1)}, bf16[160,256]{1,0:T(8,128)(2,1)S(1)}, u32[]{:S(2)}, u32[]{:S(2)}) collective-permute-start(bf16[160,256]{1,0:T(8,128)(2,1)S(1)} %bitcast.134), channel_id=1, source_target_pairs={{0,8},{4,12},{8,0},{12,4},{16,24},{20,28},{24,16},{28,20},{1,9},{5... | collective-permute-start | bytes 245768 | tf_op jit(solution)/shard_map/ppermute | solution.py:29
  53.2 10.3 %collective-permute-start.22 = (bf16[160,256]{1,0:T(8,128)(2,1)S(1)}, bf16[160,256]{1,0:T(8,128)(2,1)S(1)}, u32[]{:S(2)}, u32[]{:S(2)}) collective-permute-start(bf16[160,256]{1,0:T(8,128)(2,1)S(1)} %bitcast.135), channel_id=1, source_target_pairs={{0,4},{4,0},{8,12},{12,8},{16,20},{20,16},{24,28},{28,24},{1,5},{5... | collective-permute-start | bytes 245768 | tf_op jit(solution)/shard_map/ppermute | solution.py:29
  54.9 13.3 %collective-permute-start.24 = (bf16[352,256]{1,0:T(8,128)(2,1)S(1)}, bf16[352,256]{1,0:T(8,128)(2,1)S(1)}, u32[]{:S(2)}, u32[]{:S(2)}) collective-permute-start(bf16[352,256]{1,0:T(8,128)(2,1)S(1)} %pad_maximum_fusion.5), channel_id=1, source_target_pairs={{0,16},{4,20},{8,24},{12,28},{16,0},{20,4},{24,8},{28,12},{1,17},{... | collective-permute-start | bytes 540680 | tf_op jit(solution)/shard_map/ppermute | solution.py:29
  63.6 5.6 collective-permute-start.23
  132.0 13.3 %collective-permute-start.1 = (bf16[1024,256]{0,1:T(8,128)(2,1)S(1)}, bf16[1024,256]{0,1:T(8,128)(2,1)S(1)}, u32[]{:S(2)}, u32[]{:S(2)}) collective-permute-start(bf16[1024,256]{0,1:T(8,128)(2,1)S(1)} %pad_maximum_fusion.1), channel_id=1, source_target_pairs={{0,2},{1,3},{2,0},{3,1},{4,6},{5,7},{6,4},{7,5},{8,10},{9,11},{10,... | collective-permute-start | bytes 1572872 | tf_op jit(solution)/shard_map/cond/branch_0_fun/ppermute | solution.py:29
  133.8 11.4 %collective-permute-start = (bf16[1024,256]{0,1:T(8,128)(2,1)S(1)}, bf16[1024,256]{0,1:T(8,128)(2,1)S(1)}, u32[]{:S(2)}, u32[]{:S(2)}) collective-permute-start(bf16[1024,256]{0,1:T(8,128)(2,1)S(1)} %pad_maximum_fusion.1), channel_id=1, source_target_pairs={{0,1},{1,0},{2,3},{3,2},{4,5},{5,4},{6,7},{7,6},{8,9},{9,8},{10,11... | collective-permute-start | bytes 1572872 | tf_op jit(solution)/shard_map/cond/branch_0_fun/ppermute | solution.py:29
  145.2 2.0 collective-permute-start.2
  145.2 0.8 copy-start.5
  218.8 69.7 %copy-start.1 = (f32[8,256,512]{2,1,0:T(8,128)S(1)}, f32[8,256,512]{2,1,0:T(8,128)}, u32[]{:S(2)}) copy-start(f32[8,256,512]{2,1,0:T(8,128)} %get-tuple-element.173) | copy-start | bytes 12582916 | tf_op jit(solution)/shard_map/cond
  220.8 67.7 %collective-permute-start.3 = (f32[4,256,512]{2,1,0:T(8,128)S(1)}, f32[4,256,512]{2,1,0:T(8,128)S(1)}, u32[]{:S(2)}, u32[]{:S(2)}) collective-permute-start(f32[4,256,512]{2,1,0:T(8,128)S(1)} %slice.118), channel_id=1, source_target_pairs={{0,16},{4,20},{8,24},{12,28},{16,0},{20,4},{24,8},{28,12},{1,17},{... | collective-permute-start | bytes 6291464 | tf_op jit(solution)/shard_map/cond/branch_0_fun/ppermute | solution.py:29
  289.0 372.6 %collective-permute-start.4 = (f32[2,256,512]{2,1,0:T(8,128)S(1)}, f32[2,256,512]{2,1,0:T(8,128)S(1)}, u32[]{:S(2)}, u32[]{:S(2)}) collective-permute-start(f32[2,256,512]{2,1,0:T(8,128)S(1)} %slice.178), channel_id=1, source_target_pairs={{0,8},{4,12},{8,0},{12,4},{16,24},{20,28},{24,16},{28,20},{1,9},{5... | collective-permute-start | bytes 3145736 | tf_op jit(solution)/shard_map/cond/branch_0_fun/ppermute | solution.py:29
  661.8 14.0 %collective-permute-start.5 = (f32[1,256,512]{2,1,0:T(8,128)S(1)}, f32[1,256,512]{2,1,0:T(8,128)S(1)}, u32[]{:S(2)}, u32[]{:S(2)}) collective-permute-start(f32[1,256,512]{2,1,0:T(8,128)S(1)} %slice.180), channel_id=1, source_target_pairs={{0,4},{4,0},{8,12},{12,8},{16,20},{20,16},{24,28},{28,24},{1,5},{5... | collective-permute-start | bytes 1572872 | tf_op jit(solution)/shard_map/cond/branch_0_fun/ppermute | solution.py:29
  676.2 0.8 copy-start.4

commit v2 on v1

--- a/solution.py
+++ b/solution.py
@@ -17,7 +17,7 @@
 EARLY_COST = 1024
 LATE_COST = 1024
 FACTOR_COST = 200 * 2**20
-CHUNKS = (176, 80)
+CHUNKS = (192, 64)
 NEWTON = 2
 
 

time: 678 us -> 680 us (level)
  the two profiles are of different devices: /device:TPU:2 before, /device:TPU:0 now
where the time goes in v2:
time: 680 us; the launch traced here: 683 us
  starting transfers between devices  431 us (63%)
  waiting for transfers between devices  106 us (16%)
  other arithmetic  58.5 us (9%)
  loops' own time  32.1 us (5%)
  local copies, waits for them, and re-layouts  26.4 us (4%)
  Pallas kernels  14.2 us (2%)
  matrix products  13.1 us (2%)
    ppermute x25, starting transfers between devices, swap(): return lax.ppermute(x, axis, [(i, i ^ bit) for i in range(count)])  431 us
    ppermute x25, waiting for transfers between devices, swap(): return lax.ppermute(x, axis, [(i, i ^ bit) for i in range(count)])  106 us
    another operation x6, other arithmetic, full_path(): lower = jnp.linalg.cholesky(gram)  34.1 us
    another operation x1, loops' own time, full_path(): totals = lax.fori_loop(0, tile_count[0], step, totals)  30.1 us
    another operation x5, other arithmetic, full_path(): lax.linalg.triangular_solve(lower, sketch, left_side=False, lower=True, t...  19.8 us
  transfers between devices with their start and end apart: 25, of which 17 were waited for; matrix products, arithmetic and copies ran while one was open for 0% of the time, Pallas kernels for 2%

profile of v2, /device:TPU:0, one launch (start us, length us, event | category | flops | bytes accessed | tf_op | source)
XLA Modules:
  0.0 683.0 jit_solution(2168880335160532489)
XLA Ops:
  0.0 1.2 copy-done
  2.1 2.6 collective-permute-start.11
  4.7 1.4 shard_map.67
  7.6 1.6 collective-permute-start.7
  10.0 2.9 shard_map.68
  13.3 9.5 %collective-permute-done.11.refs_0_ = bf16[384,1024]{1,0:T(8,128)(2,1)S(1)} collective-permute-done((bf16[384,1024]{1,0:T(8,128)(2,1)S(1)}, bf16[384,1024]{1,0:T(8,128)(2,1)S(1)}, u32[]{:S(2)}, u32[]{:S(2)}) %collective-permute-start.11) | collective-permute-done | bytes 786464 | tf_op jit(solution)/shard_map/ppermute | solution.py:29
  22.8 2.9 collective-permute-start.10
  25.7 1.5 collective-permute-start.16
  27.2 3.1 shard_map.69
  30.3 2.5 collective-permute-done.10
  32.8 1.6 collective-permute-start.14
  34.4 3.3 collective-permute-start.15
  37.9 1.4 collective-permute-done.17.refs_1_
  39.3 2.6 shard_map.70
  41.9 1.9 collective-permute-done.13
  46.1 1.7 collective-permute-start.19
  48.5 6.5 collective-permute-done.20
  56.5 1.8 collective-permute-start.22
  58.4 3.4 collective-permute-start.24
  61.7 3.8 shard_map.71
  66.4 3.9 collective-permute-done.24
  70.4 1.8 collective-permute-done.23
  72.2 610.0 %conditional.1 = (f32[1,1,256,512]{3,2,1,0:T(8,128)S(1)}) conditional(s32[]{:T(128)} %bitcast.36, (s32[1]{0:T(128)}, f32[264,128]{1,0:T(8,128)S(1)}, f32[256,1024]{1,0:T(8,128)S(1)}, s32[1,8]{1,0:T(1,128)S(1)}, s32[40]{0:T(128)S(1)}, /*index=5*/s32[40]{0:T(128)S(1)}, bf16[40,512,512]{2,1,0:T(8,128)(2,1)}) %tuple.91, (f32[2,64,256]{2,1,0:T(8,128)S(1)}, ...), branch_computations={%region_0.7_spmd, %region_7.8_spmd} | conditional | flops 802537728 | bytes 80229168 | solution.py:489
  72.9 11.7 %cholesky.8 = f32[128,128]{1,0:T(8,128)S(1)} custom-call(f32[128,128]{1,0:T(8,128)S(1)} %cholesky.47), custom_call_target="Cholesky" | custom-call | tf_op jit(solution)/shard_map/cond/branch_0_fun/jit(cholesky)/cholesky | solution.py:354
  84.9 9.8 %custom-call.12 = f32[1,128,128]{1,2,0:T(8,128)S(1)} custom-call(f32[1,128,128]{2,1,0:T(8,128)S(1)} %copy.15), custom_call_target="InvertDiagBlocksLowerTriangular" | custom-call | tf_op jit(solution)/shard_map/cond/branch_0_fun/jit(cholesky)/cholesky | solution.py:354
  95.2 11.7 %cholesky.30 = f32[128,128]{1,0:T(8,128)S(1)} custom-call(f32[128,128]{1,0:T(8,128)S(1)} %convolution_subtract_fusion.1), custom_call_target="Cholesky" | custom-call | tf_op jit(solution)/shard_map/cond/branch_0_fun/jit(cholesky)/cholesky | solution.py:354
  109.2 4.1 while.13
  110.0 1.3 bitcast_dynamic-update-slice_fusion.2
  111.9 1.3 bitcast_dynamic-update-slice_fusion.2
  113.2 19.7 %custom-call.13 = f32[2,128,128]{1,2,0:T(8,128)S(1)} custom-call(f32[2,128,128]{2,1,0:T(8,128)S(1)} %get-tuple-element.267), custom_call_target="InvertDiagBlocksLowerTriangular" | custom-call | tf_op jit(solution)/shard_map/cond/branch_0_fun/triangular_solve | solution.py:355
  134.9 1.6 collective-permute-start.1
  136.4 10.8 %collective-permute-done.1 = bf16[1024,256]{0,1:T(8,128)(2,1)S(1)} collective-permute-done((bf16[1024,256]{0,1:T(8,128)(2,1)S(1)}, bf16[1024,256]{0,1:T(8,128)(2,1)S(1)}, u32[]{:S(2)}, u32[]{:S(2)}) %collective-permute-start.1) | collective-permute-done | bytes 524320 | tf_op jit(solution)/shard_map/cond/branch_0_fun/ppermute | solution.py:29
  148.1 1.2 collective-permute-done.2
  149.3 3.1 pad_maximum_fusion
  152.4 2.5 broadcast.96
  154.9 55.1 %while.12 = (s32[]{:T(128)}, f32[8,256,512]{2,1,0:T(8,128)}, s32[]{:T(128)}, s32[40]{0:T(128)S(1)}, s32[8]{0:T(128)S(1)}, /*index=5*/s32[]{:T(128)}, s32[40]{0:T...) while((s32[]{:T(128)}, f32[8,256,512]{2,1,0:T(8,128)}, ...), condition=%wide.region_6.6_spmd, body=%wide.region_5.5_spmd.sunk | while | flops 134348832 | bytes 2884192 | solution.py:377
  162.6 1.1 constant_dynamic-slice_fusion.4
  163.6 2.1 fusion.30
  173.4 1.1 constant_dynamic-slice_fusion.4
  174.5 2.1 fusion.30
  185.4 2.1 fusion.30
  196.3 2.1 fusion.30
  207.2 2.2 fusion.30
  210.0 1.9 slice.118
  212.0 26.9 %collective-permute-done.3 = f32[4,256,512]{2,1,0:T(8,128)S(1)} collective-permute-done((f32[4,256,512]{2,1,0:T(8,128)S(1)}, f32[4,256,512]{2,1,0:T(8,128)S(1)}, u32[]{:S(2)}, u32[]{:S(2)}) %collective-permute-start.3) | collective-permute-done | bytes 2097184 | tf_op jit(solution)/shard_map/cond/branch_0_fun/ppermute | solution.py:29
  239.5 406.2 %collective-permute-start.4 = (f32[2,256,512]{2,1,0:T(8,128)S(1)}, f32[2,256,512]{2,1,0:T(8,128)S(1)}, u32[]{:S(2)}, u32[]{:S(2)}) collective-permute-start(f32[2,256,512]{2,1,0:T(8,128)S(1)} %slice.178), channel_id=1, source_target_pairs={{0,8},{4,12},{8,0},{12,4},{16,24},{20,28},{24,16},{28,20},{1,9},{5... | collective-permute-start | bytes 3145736 | tf_op jit(solution)/shard_map/cond/branch_0_fun/ppermute | solution.py:29
  645.7 23.0 %collective-permute-done.4 = f32[2,256,512]{2,1,0:T(8,128)S(1)} collective-permute-done((f32[2,256,512]{2,1,0:T(8,128)S(1)}, f32[2,256,512]{2,1,0:T(8,128)S(1)}, u32[]{:S(2)}, u32[]{:S(2)}) %collective-permute-start.4) | collective-permute-done | bytes 1048608 | tf_op jit(solution)/shard_map/cond/branch_0_fun/ppermute | solution.py:29
  669.0 12.9 %collective-permute-done.5 = f32[1,256,512]{2,1,0:T(8,128)S(1)} collective-permute-done((f32[1,256,512]{2,1,0:T(8,128)S(1)}, f32[1,256,512]{2,1,0:T(8,128)S(1)}, u32[]{:S(2)}, u32[]{:S(2)}) %collective-permute-start.5) | collective-permute-done | bytes 524320 | tf_op jit(solution)/shard_map/cond/branch_0_fun/ppermute | solution.py:29
  (132 shorter events, 27.8 us)
Async XLA Ops:
  0.0 1.2 copy-start
  1.6 6.0 copy-start.2
  1.6 8.3 %collective-permute-start.8 = (bf16[384,1024]{1,0:T(8,128)(2,1)S(1)}, bf16[384,1024]{1,0:T(8,128)(2,1)S(1)}, u32[]{:S(2)}, u32[]{:S(2)}) collective-permute-start(bf16[384,1024]{1,0:T(8,128)(2,1)S(1)} %get-tuple-element.221.refs_0_), channel_id=1, source_target_pairs={{0,1},{1,0},{2,3},{3,2},{4,5},{5,4},{6,7},{7,6},{8,9},{9,8},{10,11... | collective-permute-start | bytes 2359304 | tf_op jit(solution)/shard_map/ppermute | solution.py:29
  2.1 20.7 %collective-permute-start.11 = (bf16[384,1024]{1,0:T(8,128)(2,1)S(1)}, bf16[384,1024]{1,0:T(8,128)(2,1)S(1)}, u32[]{:S(2)}, u32[]{:S(2)}) collective-permute-start(bf16[384,1024]{1,0:T(8,128)(2,1)S(1)} %get-tuple-element.221.refs_0_), channel_id=1, source_target_pairs={{0,2},{1,3},{2,0},{3,1},{4,6},{5,7},{6,4},{7,5},{8,10},{9,11},{10,... | collective-permute-start | bytes 2359304 | tf_op jit(solution)/shard_map/ppermute | solution.py:29
  6.1 1.4 collective-permute-start.6
  6.3 3.6 collective-permute-start.9
  7.6 5.7 collective-permute-start.7
  9.9 17.2 %copy-start.6 = (s32[1,8]{1,0:T(1,128)S(1)}, s32[1,8]{1,0:T(1,128)}, u32[]{:S(2)}) copy-start(s32[1,8]{1,0:T(1,128)} %param.15) | copy-start | bytes 100
  9.9 17.2 %copy-start.7 = (s32[40]{0:T(128)S(1)}, s32[40]{0:T(128)}, u32[]{:S(2)}) copy-start(s32[40]{0:T(128)} %items.5) | copy-start | bytes 484
  10.0 17.2 %copy-start.8 = (s32[40]{0:T(128)S(1)}, s32[40]{0:T(128)}, u32[]{:S(2)}) copy-start(s32[40]{0:T(128)} %users.5) | copy-start | bytes 484
  22.8 4.4 collective-permute-start.12
  22.8 10.0 %collective-permute-start.10 = (f32[264,128]{1,0:T(8,128)S(1)}, f32[264,128]{1,0:T(8,128)S(1)}, u32[]{:S(2)}, u32[]{:S(2)}) collective-permute-start(f32[264,128]{1,0:T(8,128)S(1)} %add.135), channel_id=1, source_target_pairs={{0,16},{4,20},{8,24},{12,28},{16,0},{20,4},{24,8},{28,12},{1,17},{... | collective-permute-start | bytes 405512 | tf_op jit(solution)/shard_map/ppermute | solution.py:29
  25.7 12.0 %collective-permute-start.16 = (bf16[128,1024]{1,0:T(8,128)(2,1)S(1)}, bf16[128,1024]{1,0:T(8,128)(2,1)S(1)}, u32[]{:S(2)}, u32[]{:S(2)}) collective-permute-start(bf16[128,1024]{1,0:T(8,128)(2,1)S(1)} %get-tuple-element.222.refs_1_), channel_id=1, source_target_pairs={{0,2},{1,3},{2,0},{3,1},{4,6},{5,7},{6,4},{7,5},{8,10},{9,11},{10,... | collective-permute-start | bytes 786440 | tf_op jit(solution)/shard_map/ppermute | solution.py:29
  32.8 11.0 %collective-permute-start.14 = (bf16[768,256]{1,0:T(8,128)(2,1)S(1)}, bf16[768,256]{1,0:T(8,128)(2,1)S(1)}, u32[]{:S(2)}, u32[]{:S(2)}) collective-permute-start(bf16[768,256]{1,0:T(8,128)(2,1)S(1)} %bitcast.122), channel_id=1, source_target_pairs={{0,4},{4,0},{8,12},{12,8},{16,20},{20,16},{24,28},{28,24},{1,5},{5... | collective-permute-start | bytes 1179656 | tf_op jit(solution)/shard_map/ppermute | solution.py:29
  34.4 10.5 %collective-permute-start.15 = (bf16[768,256]{1,0:T(8,128)(2,1)S(1)}, bf16[768,256]{1,0:T(8,128)(2,1)S(1)}, u32[]{:S(2)}, u32[]{:S(2)}) collective-permute-start(bf16[768,256]{1,0:T(8,128)(2,1)S(1)} %bitcast.121), channel_id=1, source_target_pairs={{0,8},{4,12},{8,0},{12,4},{16,24},{20,28},{24,16},{28,20},{1,9},{5... | collective-permute-start | bytes 1179656 | tf_op jit(solution)/shard_map/ppermute | solution.py:29
  37.7 1.6 collective-permute-start.17
  37.8 6.0 collective-permute-start.13
  45.0 9.9 %collective-permute-start.20 = (bf16[640,256]{1,0:T(8,128)(2,1)S(1)}, bf16[640,256]{1,0:T(8,128)(2,1)S(1)}, u32[]{:S(2)}, u32[]{:S(2)}) collective-permute-start(bf16[640,256]{1,0:T(8,128)(2,1)S(1)} %pad_maximum_fusion.4), channel_id=1, source_target_pairs={{0,4},{4,0},{8,12},{12,8},{16,20},{20,16},{24,28},{28,24},{1,5},{5... | collective-permute-start | bytes 983048 | tf_op jit(solution)/shard_map/ppermute | solution.py:29
  46.1 9.1 %collective-permute-start.19 = (bf16[640,256]{1,0:T(8,128)(2,1)S(1)}, bf16[640,256]{1,0:T(8,128)(2,1)S(1)}, u32[]{:S(2)}, u32[]{:S(2)}) collective-permute-start(bf16[640,256]{1,0:T(8,128)(2,1)S(1)} %pad_maximum_fusion.3), channel_id=1, source_target_pairs={{0,8},{4,12},{8,0},{12,4},{16,24},{20,28},{24,16},{28,20},{1,9},{5... | collective-permute-start | bytes 983048 | tf_op jit(solution)/shard_map/ppermute | solution.py:29
  47.9 8.5 %collective-permute-start.18 = (f32[264,128]{1,0:T(8,128)S(1)}, f32[264,128]{1,0:T(8,128)S(1)}, u32[]{:S(2)}, u32[]{:S(2)}) collective-permute-start(f32[264,128]{1,0:T(8,128)S(1)} %add.137), channel_id=1, source_target_pairs={{0,4},{4,0},{8,12},{12,8},{16,20},{20,16},{24,28},{28,24},{1,5},{5... | collective-permute-start | bytes 405512 | tf_op jit(solution)/shard_map/ppermute | solution.py:29
  55.0 17.2 %copy-start.3 = (f32[256,1024]{1,0:T(8,128)S(1)}, f32[256,1024]{1,0:T(8,128)}, u32[]{:S(2)}) copy-start(f32[256,1024]{1,0:T(8,128)} %copy-done.2) | copy-start | bytes 3145732
  56.5 9.7 %collective-permute-start.21 = (bf16[128,256]{1,0:T(8,128)(2,1)S(1)}, bf16[128,256]{1,0:T(8,128)(2,1)S(1)}, u32[]{:S(2)}, u32[]{:S(2)}) collective-permute-start(bf16[128,256]{1,0:T(8,128)(2,1)S(1)} %bitcast.136), channel_id=1, source_target_pairs={{0,8},{4,12},{8,0},{12,4},{16,24},{20,28},{24,16},{28,20},{1,9},{5... | collective-permute-start | bytes 196616 | tf_op jit(solution)/shard_map/ppermute | solution.py:29
  56.5 9.7 %collective-permute-start.22 = (bf16[128,256]{1,0:T(8,128)(2,1)S(1)}, bf16[128,256]{1,0:T(8,128)(2,1)S(1)}, u32[]{:S(2)}, u32[]{:S(2)}) collective-permute-start(bf16[128,256]{1,0:T(8,128)(2,1)S(1)} %bitcast.137), channel_id=1, source_target_pairs={{0,4},{4,0},{8,12},{12,8},{16,20},{20,16},{24,28},{28,24},{1,5},{5... | collective-permute-start | bytes 196616 | tf_op jit(solution)/shard_map/ppermute | solution.py:29
  58.4 11.9 %collective-permute-start.24 = (bf16[384,256]{1,0:T(8,128)(2,1)S(1)}, bf16[384,256]{1,0:T(8,128)(2,1)S(1)}, u32[]{:S(2)}, u32[]{:S(2)}) collective-permute-start(bf16[384,256]{1,0:T(8,128)(2,1)S(1)} %pad_maximum_fusion.5), channel_id=1, source_target_pairs={{0,16},{4,20},{8,24},{12,28},{16,0},{20,4},{24,8},{28,12},{1,17},{... | collective-permute-start | bytes 589832 | tf_op jit(solution)/shard_map/ppermute | solution.py:29
  66.3 5.9 collective-permute-start.23
  134.9 12.4 %collective-permute-start.1 = (bf16[1024,256]{0,1:T(8,128)(2,1)S(1)}, bf16[1024,256]{0,1:T(8,128)(2,1)S(1)}, u32[]{:S(2)}, u32[]{:S(2)}) collective-permute-start(bf16[1024,256]{0,1:T(8,128)(2,1)S(1)} %pad_maximum_fusion.1), channel_id=1, source_target_pairs={{0,2},{1,3},{2,0},{3,1},{4,6},{5,7},{6,4},{7,5},{8,10},{9,11},{10,... | collective-permute-start | bytes 1572872 | tf_op jit(solution)/shard_map/cond/branch_0_fun/ppermute | solution.py:29
  136.4 10.9 %collective-permute-start = (bf16[1024,256]{0,1:T(8,128)(2,1)S(1)}, bf16[1024,256]{0,1:T(8,128)(2,1)S(1)}, u32[]{:S(2)}, u32[]{:S(2)}) collective-permute-start(bf16[1024,256]{0,1:T(8,128)(2,1)S(1)} %pad_maximum_fusion.1), channel_id=1, source_target_pairs={{0,1},{1,0},{2,3},{3,2},{4,5},{5,4},{6,7},{7,6},{8,9},{9,8},{10,11... | collective-permute-start | bytes 1572872 | tf_op jit(solution)/shard_map/cond/branch_0_fun/ppermute | solution.py:29
  147.3 2.0 collective-permute-start.2
  147.3 0.8 copy-start.5
  210.0 28.9 %copy-start.1 = (f32[8,256,512]{2,1,0:T(8,128)S(1)}, f32[8,256,512]{2,1,0:T(8,128)}, u32[]{:S(2)}) copy-start(f32[8,256,512]{2,1,0:T(8,128)} %get-tuple-element.173) | copy-start | bytes 12582916 | tf_op jit(solution)/shard_map/cond
  211.9 27.0 %collective-permute-start.3 = (f32[4,256,512]{2,1,0:T(8,128)S(1)}, f32[4,256,512]{2,1,0:T(8,128)S(1)}, u32[]{:S(2)}, u32[]{:S(2)}) collective-permute-start(f32[4,256,512]{2,1,0:T(8,128)S(1)} %slice.118), channel_id=1, source_target_pairs={{0,16},{4,20},{8,24},{12,28},{16,0},{20,4},{24,8},{28,12},{1,17},{... | collective-permute-start | bytes 6291464 | tf_op jit(solution)/shard_map/cond/branch_0_fun/ppermute | solution.py:29
  239.5 429.2 %collective-permute-start.4 = (f32[2,256,512]{2,1,0:T(8,128)S(1)}, f32[2,256,512]{2,1,0:T(8,128)S(1)}, u32[]{:S(2)}, u32[]{:S(2)}) collective-permute-start(f32[2,256,512]{2,1,0:T(8,128)S(1)} %slice.178), channel_id=1, source_target_pairs={{0,8},{4,12},{8,0},{12,4},{16,24},{20,28},{24,16},{28,20},{1,9},{5... | collective-permute-start | bytes 3145736 | tf_op jit(solution)/shard_map/cond/branch_0_fun/ppermute | solution.py:29
  668.9 13.0 %collective-permute-start.5 = (f32[1,256,512]{2,1,0:T(8,128)S(1)}, f32[1,256,512]{2,1,0:T(8,128)S(1)}, u32[]{:S(2)}, u32[]{:S(2)}) collective-permute-start(f32[1,256,512]{2,1,0:T(8,128)S(1)} %slice.180), channel_id=1, source_target_pairs={{0,4},{4,0},{8,12},{12,8},{16,20},{20,16},{24,28},{28,24},{1,5},{5... | collective-permute-start | bytes 1572872 | tf_op jit(solution)/shard_map/cond/branch_0_fun/ppermute | solution.py:29
  682.2 0.8 copy-start.4
